TPU v7x, 32 devices: a whole 2x2x4 slice. The times are simulated.
32 devices in a mesh: gx: 4 (over z), gy: 8 (over y, x, core).
Axes of the slice: x: 2, y: 2, z: 4, core: 2. Of those that a mesh axis runs over, the one named last changes fastest.
Arguments:
- heat_source: float32 [1536, 1024], P(('gx', 'gy')), may hold values from -18 to 18
- stiffness: float32 [512, 384, 384], P(('gx', 'gy')), may hold values from -1 to 32, as said below
- element_faces: int32 [512, 6], P(('gx', 'gy')), may hold values from 0 to 1535, as said below
Outputs:
- solution: float32 [1536, 1024], P(('gx', 'gy'))
- residual: float32 [1536, 1024], P(('gx', 'gy'))
Inputs may be any that keep to these rules, and one draw needn't show every extreme that they name: `element_faces`: the elements form a periodic grid of 8 x 16 x 4 hexahedra; device (i, j) of gx and gy holds the block of 2 x 2 x 4 elements at streamwise block i and spanwise block j, in a local order of its own, and owns the lower x, lower y and lower z faces of its elements, numbered in an order of its own. So every face number appears exactly twice, and a device's elements reference faces of itself, of the next device along gx (cyclic, same gy index; exactly 8 references) and of the next device along gy (cyclic, same gx index; exactly 8 references). `stiffness`: each element matrix is symmetric with a positive diagonal and strictly diagonally dominant.
All inputs are finite; a program needn't handle non-finite values.
Results may differ from a plain program's by a relative error of at most 0.0002.
Values sent between devices are 32-bit elements; how exact they have to be, the bound alone decides.
A program may use at most 128 MiB of HBM per device.

v0:
```python
import jax
import jax.numpy as jnp
from jax import lax
from jax.experimental import pallas as pl
from jax.experimental.pallas import tpu as pltpu
from jax.sharding import PartitionSpec as P

BLOCK = 64
EX = 2
EY = 2
EZ = 4
HALF = BLOCK
LANES = 2 * BLOCK
F32 = jnp.float32
BF16 = jnp.bfloat16
MESH = pl.DeviceIdType.MESH
UNROLL = 2


def index_tables(faces, base, count, face_dev, nx, ny, idx):
    sub = lax.broadcasted_iota(jnp.int32, (count, count), 0)
    lane = lax.broadcasted_iota(jnp.int32, (count, count), 1)
    eye = sub == lane
    slots = 6 * count
    rows = [faces[k : k + 1, :] for k in range(6)]
    cols = [jnp.sum(jnp.where(eye, r, 0), axis=1, keepdims=True) for r in rows]
    idx[...] = jnp.zeros(idx.shape, jnp.int32)
    sizes = [nx, nx, ny, ny]
    starts = [slots, slots + nx, slots + 2 * nx, slots + 2 * nx + ny]
    for axis in range(3):
        low, up = 2 * axis, 2 * axis + 1
        for k, other in ((low, up), (up, low)):
            match = (cols[other] == rows[k]).astype(jnp.int32)
            has = jnp.sum(match, axis=0, keepdims=True)
            place = jnp.sum(match * (other * count + sub), axis=0, keepdims=True)
            local = rows[k] - base
            if axis == 2:
                idx[k : k + 1, 0:count] = place
                idx[6 + k : 7 + k, 0:count] = local
                continue
            match_c = (cols[k] == rows[other]).astype(jnp.int32)
            has_c = jnp.sum(match_c, axis=1, keepdims=True)
            before = jnp.where((has_c == 0) & (cols[k] < rows[k]), 1, 0)
            rank = jnp.sum(before, axis=0, keepdims=True)
            before_c = jnp.where((has == 0) & (rows[k] < cols[k]), 1, 0)
            rank_c = jnp.sum(before_c, axis=1, keepdims=True)
            chosen = (has_c == 0) & (rank_c == lane)
            listed = jnp.sum(jnp.where(chosen, k * count + sub, 0), axis=0, keepdims=True)
            idx[k : k + 1, 0:count] = jnp.where(has > 0, place, starts[k] + rank)
            if k == low:
                traces = jnp.where(chosen, cols[k] - base, 0)
                idx[17 + axis : 18 + axis, 0:count] = jnp.sum(traces, axis=0, keepdims=True)
                idx[6 + k : 7 + k, 0:count] = local
            else:
                first = face_dev + (0 if axis == 0 else nx)
                idx[6 + k : 7 + k, 0:count] = jnp.where(has > 0, local, first + rank)
            idx[12 + k : 13 + k, 0:count] = listed
    wide = lax.broadcasted_iota(jnp.int32, (count, LANES), 1)
    wide_sub = lax.broadcasted_iota(jnp.int32, (count, LANES), 0)
    inverse = jnp.zeros((1, LANES), jnp.int32)
    for k in (0, 2, 4):
        owned = (cols[k] - base) == wide
        inverse = inverse + jnp.sum(
            jnp.where(owned, k * count + wide_sub, 0), axis=0, keepdims=True
        )
    idx[16:17, :] = inverse
    idx[0:6, :] = jnp.clip(idx[0:6, :], 0, slots + 2 * (nx + ny) - 1)
    idx[6:12, :] = jnp.clip(idx[6:12, :], 0, face_dev + nx + ny - 1)
    idx[12:17, :] = jnp.clip(idx[12:17, :], 0, slots - 1)
    idx[17:19, :] = jnp.clip(idx[17:19, :], 0, face_dev - 1)


def make_kernel(outer, inner, count, face_dev, groups, nx, ny):
    slots = 6 * count
    lows = (0, 2, 4)
    parts = outer * inner

    def kernel(heat_hbm, faces_hbm, stiff_ref, sol_ref, res_ref,
               heat_ref, faces_ref, raw, high, low, diag, tile_rows, table, v0, v1, v2, flux, flux2, q1,
               idx_v, idx, send0, recv0, sends, recvs, sum_tx, sum_rx,
               in_sem, raw_sem, idx_sem, s0_sem, r0_sem, ss_sem, rr_sem,
               sum_ss, sum_rs):
        gx = lax.axis_index("gx")
        gy = lax.axis_index("gy")
        x_next = (lax.rem(gx + 1, outer), gy)
        x_prev = (lax.rem(gx + outer - 1, outer), gy)
        y_next = (gx, lax.rem(gy + 1, inner))
        y_prev = (gx, lax.rem(gy + inner - 1, inner))

        get_heat = pltpu.make_async_copy(heat_hbm, heat_ref, in_sem.at[0])
        get_faces = pltpu.make_async_copy(faces_hbm, faces_ref, in_sem.at[1])
        get_faces.start()
        get_heat.start()

        def other(d):
            return (lax.rem(gx + d // inner, outer), lax.rem(gy + d % inner, inner))

        def raw_copy(e):
            return pltpu.make_async_copy(stiff_ref.at[e], raw.at[e], raw_sem.at[e])

        for e in range(count):
            raw_copy(e).start()
        barrier = pltpu.get_barrier_semaphore()
        for d in range(1, parts):
            pl.semaphore_signal(barrier, inc=1, device_id=other(d), device_id_type=MESH)

        base = (gx * inner + gy) * face_dev
        get_faces.wait()
        index_tables(faces_ref[...], base, count, face_dev, nx, ny, idx_v)
        to_smem = pltpu.make_async_copy(idx_v, idx, idx_sem)
        to_smem.start()
        get_heat.wait()
        for g in range(face_dev // 8):
            for j in range(groups):
                tile_rows[(g * groups + j) * 8 : (g * groups + j + 1) * 8, :] = heat_ref[
                    g * 8 : g * 8 + 8, j * LANES : (j + 1) * LANES
                ]
        for f in range(face_dev):
            start = (f // 8) * groups * 8 + f % 8
            table[f] = tile_rows[pl.ds(start, groups, stride=8), :]
        to_smem.wait()
        for r in range(nx):
            send0[r] = table[idx[17, r]]
        for r in range(ny):
            send0[nx + r] = table[idx[18, r]]
        pl.semaphore_wait(barrier, parts - 1)

        def remote(src, dst, ssem, rsem, device):
            return pltpu.make_async_remote_copy(
                src_ref=src, dst_ref=dst, send_sem=ssem, recv_sem=rsem,
                device_id=device, device_id_type=MESH,
            )

        first = [
            remote(send0.at[pl.ds(0, nx)], recv0.at[pl.ds(0, nx)], s0_sem.at[0], r0_sem.at[0], x_prev),
            remote(send0.at[pl.ds(nx, ny)], recv0.at[pl.ds(nx, ny)], s0_sem.at[1], r0_sem.at[1], y_prev),
        ]
        for c in first:
            c.start()

        eye = lax.broadcasted_iota(jnp.int32, (LANES, LANES), 0) == lax.broadcasted_iota(
            jnp.int32, (LANES, LANES), 1
        )

        def split(e, carry):
            raw_copy(e).wait()
            for r in range(3):
                rows = pl.ds(r * LANES, LANES)
                for c in range(3):
                    columns = pl.ds(c * LANES, LANES)
                    a = raw[e, rows, columns]
                    if r == c:
                        diag[e, :, columns] = jnp.sum(
                            jnp.where(eye, a, 0.0), axis=0, keepdims=True
                        )
                        a = jnp.where(eye, 0.0, a)
                    h = a.astype(BF16)
                    high[e, rows, columns] = h
                    low[e, rows, columns] = (a - h.astype(F32)).astype(BF16)
            return carry

        lax.fori_loop(0, count, split, 0)
        left = lax.broadcasted_iota(jnp.int32, (8, LANES), 1) < HALF

        def swap(a):
            return pltpu.roll(a, HALF, 1)

        def product(tiles, e):
            evens, odds = [], []
            for a, b in zip(tiles[0::2], tiles[1::2]):
                evens.append(jnp.where(left, a, swap(b)))
                odds.append(jnp.where(left, swap(a), b))
            x = jnp.concatenate(
                [jnp.concatenate(evens, axis=1), jnp.concatenate(odds, axis=1)], axis=0
            )
            depth = x.shape[1]
            xh = x.astype(BF16)
            xl = (x - xh.astype(F32)).astype(BF16)
            both = jnp.concatenate([xh, xl], axis=0)
            p = jnp.dot(both, high[e, 0:depth, :], preferred_element_type=F32)
            q = jnp.dot(xh, low[e, 0:depth, :], preferred_element_type=F32)
            y = p[0:16] + (p[16:32] + q)
            own = x * diag[e, :, 0:depth]
            out = []
            for axis in range(3):
                at = slice(axis * LANES, (axis + 1) * LANES)
                part = y[:, at] + own[:, at] if axis * LANES < depth else y[:, at]
                ev, od = part[0:8], part[8:16]
                out.append(jnp.where(left, ev, swap(od)))
                out.append(jnp.where(left, swap(ev), od))
            return out

        def inside(new, tiles_of, init):
            def body(e, acc):
                tiles, acc = tiles_of(e, acc)
                for k, f in enumerate(product(tiles, e)):
                    new[k * count + e] = f
                return acc

            return lax.fori_loop(0, count, body, init, unroll=True)

        def edges(new, tiles_of, init):
            def body(e, carry):
                dot, acc = carry
                tiles, full, acc = tiles_of(e, acc)
                for k, f in enumerate(product(tiles, e)):
                    s = k * count + e
                    f = new[s] + f
                    new[s] = f
                    dot = dot + f * full[k]
                return dot, acc

            start = (jnp.zeros((8, LANES), F32), init)
            return lax.fori_loop(0, count, body, start, unroll=True)

        spots = [0, nx, 2 * nx, 2 * nx + ny]
        plan = [(0, nx, x_prev, 1), (1, nx, x_next, 0), (2, ny, y_prev, 3), (3, ny, y_next, 2)]

        def exchange(phase, flux, kinds):
            copies = []
            for kind, rows, target, lands in plan:
                if kind not in kinds:
                    continue
                for r in range(rows):
                    sends[phase, spots[kind] + r] = flux[idx[12 + kind, r]]
                copies.append(
                    remote(
                        sends.at[phase, pl.ds(spots[kind], rows)],
                        recvs.at[phase, pl.ds(spots[lands], rows)],
                        ss_sem.at[phase, kind], rr_sem.at[phase, lands], target,
                    )
                )
                copies[-1].start()
            return copies

        def landed(phase, flux, copies, kinds):
            for c in copies:
                c.wait_recv()
            for kind, rows, _, _ in plan:
                if kind in kinds:
                    for r in range(rows):
                        flux[slots + spots[kind] + r] = recvs[phase, spots[kind] + r]

        def halves(tile):
            even = jnp.sum(jnp.where(left, tile, 0.0), axis=1, keepdims=True)
            odd = jnp.sum(jnp.where(left, 0.0, tile), axis=1, keepdims=True)
            return even, odd

        lane = lax.broadcasted_iota(jnp.int32, (8, LANES), 1)

        sub = lax.broadcasted_iota(jnp.int32, (8, LANES), 0)
        spot = lane % 16
        mine = lane // 16 == sub

        def packed(tiles, out=None, first=0):
            out = jnp.zeros((8, LANES), F32) if out is None else out
            for m, t in enumerate(tiles, first):
                even, odd = halves(t)
                out = jnp.where(spot == 2 * m, even, out)
                out = jnp.where(spot == 2 * m + 1, odd, out)
            return out

        def unpacked(row, m):
            own = jnp.where(mine, jnp.broadcast_to(row, (8, LANES)), 0.0)
            even = jnp.sum(jnp.where(spot == 2 * m, own, 0.0), axis=1, keepdims=True)
            odd = jnp.sum(jnp.where(spot == 2 * m + 1, own, 0.0), axis=1, keepdims=True)
            return jnp.where(left, even, odd)

        def sum_start(turn, value):
            sum_tx[turn] = jnp.sum(jnp.where(mine, value, 0.0), axis=0, keepdims=True)
            copies = []
            for d in range(1, parts):
                copies.append(remote(sum_tx.at[turn], sum_rx.at[turn, d - 1], sum_ss.at[turn, d - 1],
                                     sum_rs.at[turn, d - 1], other(d)))
                copies[-1].start()
            return copies

        def sum_end(turn, copies):
            for c in copies:
                c.wait_recv()
            return sum_tx[turn] + jnp.sum(sum_rx[turn], axis=0)

        zero = jnp.zeros((8, LANES), F32)

        every = (0, 1, 2, 3)

        def traces_in(e, acc):
            tiles = []
            for k in range(6):
                at = idx[6 + k, e]
                t = table[at]
                if k in (1, 3):
                    t = jnp.where(at < face_dev, t, 0.0)
                if k in lows:
                    acc = acc + t * t
                v0[k * count + e] = t
                tiles.append(t)
            return tiles, acc

        def traces_edge(e, acc):
            tiles, full = [], [v0[k * count + e] for k in range(6)]
            for k in range(4):
                t = zero
                if k in (1, 3):
                    at = idx[6 + k, e]
                    t = jnp.where(at < face_dev, 0.0, table[at])
                    full[k] = full[k] + t
                    v0[k * count + e] = full[k]
                tiles.append(t)
            return tiles, full, acc

        gamma0 = inside(flux, traces_in, zero)
        for c in first:
            c.wait_recv()
        for r in range(nx + ny):
            table[face_dev + r] = recv0[r]
        delta0, _ = edges(flux, traces_edge, 0)
        swap1 = exchange(0, flux, every)
        sum1 = sum_start(0, packed([gamma0, delta0]))

        def one_in(e, acc):
            tiles = []
            for k in range(6):
                s = k * count + e
                at = idx[k, e]
                t = flux[s] + flux[at]
                if k < 4:
                    t = jnp.where(at < slots, t, 0.0)
                v1[s] = t
                tiles.append(t)
            return tiles, acc

        def one_edge(e, acc):
            tiles, full = [], [v1[k * count + e] for k in range(6)]
            for k in range(4):
                s = k * count + e
                at = idx[k, e]
                t = jnp.where(at < slots, 0.0, flux[s] + flux[at])
                full[k] = full[k] + t
                v1[s] = full[k]
                tiles.append(t)
            return tiles, full, acc

        inside(flux2, one_in, 0)
        landed(0, flux, swap1, every)
        dot_g, _ = edges(flux2, one_edge, 0)
        swap2 = exchange(1, flux2, every)
        total = sum_end(0, sum1)
        gamma0 = unpacked(total, 0)
        delta0 = unpacked(total, 1)
        alpha0 = gamma0 / delta0

        def dots_of(s, val, w, acc):
            one = v1[s]
            r1 = v0[s] - alpha0 * one
            terms = (r1 * r1, r1 * w, w * w, w * one, one * one, w * val)
            return tuple(a + t for a, t in zip(acc, terms))

        def two_in(e, acc):
            tiles = []
            for k in range(6):
                s = k * count + e
                at = idx[k, e]
                val = flux2[s] + flux2[at]
                w = v1[s] - alpha0 * val
                if k < 4:
                    w = jnp.where(at < slots, w, 0.0)
                if k == 4:
                    acc = dots_of(s, val, w, acc)
                v2[s] = val
                q1[s] = w
                tiles.append(w)
            return tiles, acc

        def two_edge(e, acc):
            tiles, full = [], [q1[k * count + e] for k in range(6)]
            for k in range(4):
                s = k * count + e
                at = idx[k, e]
                val = flux2[s] + flux2[at]
                w = v1[s] - alpha0 * val
                tiles.append(jnp.where(at < slots, 0.0, w))
                full[k] = w
                if k in lows:
                    v2[s] = val
                    acc = dots_of(s, val, w, acc)
            return tiles, full, acc

        dots = inside(flux, two_in, (zero,) * 6)
        landed(1, flux2, swap2, every)
        dot_e, dots = edges(flux, two_edge, dots)
        early = packed([*dots, dot_g])
        sum2 = sum_start(1, packed([dot_e], early, 7))
        swap3 = exchange(2, flux, (1, 3))
        landed(2, flux, swap3, (0, 2))

        def asm3(e, carry):
            for k in lows:
                s = k * count + e
                flux[s] = flux[s] + flux[idx[k, e]]
            return carry

        lax.fori_loop(0, count, asm3, 0, unroll=UNROLL)
        total = sum_end(1, sum2)
        g1, d1, ww, wv, vv, f, g, ee = [unpacked(total, m) for m in range(8)]
        rv = -g1 / alpha0
        b0 = g1 / gamma0
        pap = d1 + 2.0 * b0 * rv + b0 * b0 * delta0
        a1 = g1 / pap
        rs = d1 + b0 * rv
        s2 = ww + b0 * (2.0 * wv + b0 * vv)
        g2 = g1 - 2.0 * a1 * rs + a1 * a1 * s2
        b1 = g2 / g1
        rar = d1 - 2.0 * a1 * (ww + b0 * wv) + a1 * a1 * (ee + b0 * (2.0 * f + b0 * g))
        pap2 = rar + 2.0 * b1 * (rs - a1 * s2) + b1 * b1 * pap
        a2 = g2 / pap2

        def finish(fc, carry):
            s = idx[16, fc]
            x0 = v0[s]
            one = v1[s]
            two = v2[s]
            r1 = x0 - alpha0 * one
            w = one - alpha0 * two
            p1 = r1 + b0 * x0
            s1 = w + b0 * one
            r2 = r1 - a1 * s1
            w2 = w - a1 * (flux[s] + b0 * two)
            p2 = r2 + b1 * p1
            sol_ref[fc] = alpha0 * x0 + a1 * p1 + a2 * p2
            res_ref[fc] = r2 - a2 * (w2 + b1 * s1)
            return carry

        lax.fori_loop(0, face_dev, finish, 0, unroll=2)
        for c in [*first, *swap1, *swap2, *swap3, *sum1, *sum2]:
            c.wait_send()

    return kernel


def local(heat_source, stiffness, element_faces):
    face_dev, width = heat_source.shape
    count, order = stiffness.shape[0], stiffness.shape[1]
    groups = width // LANES
    outer = lax.axis_size("gx")
    inner = lax.axis_size("gy")
    nx, ny = EY * EZ, EX * EZ
    slots = 6 * count
    ext = 2 * (nx + ny)
    tile = (groups, LANES)
    vmem = lambda *s: pltpu.VMEM(s, F32)
    dma = lambda *s: pltpu.SemaphoreType.DMA(s)
    out = jax.ShapeDtypeStruct((face_dev, *tile), F32)
    sol, res = pl.pallas_call(
        make_kernel(outer, inner, count, face_dev, groups, nx, ny),
        name="cg",
        out_shape=(out, out),
        in_specs=[
            pl.BlockSpec(memory_space=pltpu.HBM),
            pl.BlockSpec(memory_space=pltpu.HBM),
            pl.BlockSpec(memory_space=pltpu.HBM),
        ],
        out_specs=(pl.BlockSpec(memory_space=pltpu.VMEM),) * 2,
        scratch_shapes=[
            vmem(face_dev, width),
            pltpu.VMEM((6, count), jnp.int32),
            vmem(count, order, order),
            pltpu.VMEM((count, order, order), BF16),
            pltpu.VMEM((count, order, order), BF16),
            vmem(count, 1, order),
            vmem(face_dev * groups, LANES),
            vmem(face_dev + nx + ny, *tile),
            vmem(slots, *tile),
            vmem(slots, *tile),
            vmem(slots, *tile),
            vmem(slots + ext, *tile),
            vmem(slots + ext, *tile),
            vmem(slots, *tile),
            pltpu.VMEM((24, LANES), jnp.int32),
            pltpu.SMEM((24, LANES), jnp.int32),
            vmem(nx + ny, *tile),
            vmem(nx + ny, *tile),
            vmem(3, ext, *tile),
            vmem(3, ext, *tile),
            vmem(2, 1, LANES),
            vmem(2, outer * inner - 1, 1, LANES),
            dma(2),
            dma(count), pltpu.SemaphoreType.DMA,
            dma(2), dma(2), dma(3, 4), dma(3, 4),
            dma(2, outer * inner - 1), dma(2, outer * inner - 1),
        ],
        compiler_params=pltpu.CompilerParams(
            collective_id=0, has_side_effects=True, vmem_limit_bytes=67043328
        ),
    )(heat_source, element_faces.T, stiffness)
    return sol.reshape(face_dev, width), res.reshape(face_dev, width)


def solution(mesh):
    return jax.shard_map(
        local,
        mesh=mesh,
        in_specs=(P(("gx", "gy"), None), P(("gx", "gy"), None, None), P(("gx", "gy"), None)),
        out_specs=(P(("gx", "gy"), None), P(("gx", "gy"), None)),
        check_vma=False,
    )
```

profile of v0, /device:TPU:0, one launch (start us, length us, event | category | flops | bytes accessed | tf_op | source)
XLA Modules:
  0.0 33.2 jit_solution(3280317837006430823)
XLA Ops:
  0.6 30.7 %cg.1 = (f32[48,8,128]{2,1,0:T(8,128)}, f32[48,8,128]{2,1,0:T(8,128)}) custom-call(f32[48,1024]{1,0:T(8,128)} %heat_hbm.1, s32[6,16]{1,0:T(8,128)} %bitcast.9, f32[16,384,384]{2,1,0:T(8,128)} %stiff_ref.1), custom_call_target="tpu_custom_call" | custom-call | tf_op jit(solution)/shard_map/cg/pallas_call | solution.py:454
  31.3 1.8 %copy_bitcast_fusion = (f32[48,1024]{1,0:T(8,128)}, f32[48,1024]{1,0:T(8,128)}) fusion(f32[6,8,8,128]{3,2,1,0:T(8,128)} %bitcast.8, f32[6,8,8,128]{3,2,1,0:T(8,128)} %bitcast.7), kind=kLoop, calls=%fused_computation | loop fusion | bytes 786432 | tf_op jit(solution)/shard_map/reshape | solution.py:496
where the time goes:
time: 33.3 us; the launch traced here: 33.2 us
  Pallas kernels  30.7 us (92%)
  local copies, waits for them, and re-layouts  1.84 us (6%)
  between operations  0.64 us (2%)
    pallas_call x1, Pallas kernels, local(): pl.pallas_call(make_kernel(outer, inner, count, face_dev, groups, nx, ny)...  30.7 us
    reshape x1, local copies, waits for them, and re-layouts, local(): return (sol.reshape(face_dev, width), res.reshape(face_dev, width))  1.84 us

commit v1 on v0

v1 whole, which is shorter than its diff:
```python
import jax
import jax.numpy as jnp
from jax import lax
from jax.experimental import pallas as pl
from jax.experimental.pallas import tpu as pltpu
from jax.sharding import PartitionSpec as P

BLOCK = 64
EX = 2
EY = 2
EZ = 4
HALF = BLOCK
LANES = 2 * BLOCK
F32 = jnp.float32
BF16 = jnp.bfloat16
MESH = pl.DeviceIdType.MESH
AHEAD = 2
MIDDLE = 9


def index_tables(faces, base, count, face_dev, nx, ny, idx):
    sub = lax.broadcasted_iota(jnp.int32, (count, count), 0)
    lane = lax.broadcasted_iota(jnp.int32, (count, count), 1)
    eye = sub == lane
    slots = 6 * count
    rows = [faces[k : k + 1, :] for k in range(6)]
    cols = [jnp.sum(jnp.where(eye, r, 0), axis=1, keepdims=True) for r in rows]
    idx[...] = jnp.zeros(idx.shape, jnp.int32)
    starts = [0, nx, 2 * nx, 2 * nx + ny]
    wide = lax.broadcasted_iota(jnp.int32, (count, LANES), 1)
    wide_sub = lax.broadcasted_iota(jnp.int32, (count, LANES), 0)
    for k, other, role in ((4, 5, 1), (5, 4, 0)):
        match = (cols[other] == rows[k]).astype(jnp.int32)
        place = jnp.sum(match * sub, axis=0, keepdims=True)
        idx[1 - role : 2 - role, 0:count] = role * count + place
        idx[7 - role : 8 - role, 0:count] = rows[k] - base
    owned = (cols[4] - base) == wide
    inverse = jnp.sum(jnp.where(owned, wide_sub, 0), axis=0, keepdims=True)
    for axis in range(2):
        low, up = 2 * axis, 2 * axis + 1
        near, far = 2 + axis, 4 + axis
        match_low = (cols[up] == rows[low]).astype(jnp.int32)
        match_up = (cols[low] == rows[up]).astype(jnp.int32)
        has = jnp.sum(match_low, axis=0, keepdims=True) > 0
        has_c = jnp.sum(match_up, axis=1, keepdims=True) > 0
        partner = jnp.sum((match_low + match_up) * sub, axis=0, keepdims=True)
        idx[near : near + 1, 0:count] = near * count + partner
        idx[6 + near : 7 + near, 0:count] = jnp.where(has, rows[low], rows[up]) - base
        idx[19 + axis : 20 + axis, 0:count] = jnp.where(has, low, up)
        spot = []
        for k, away, away_c in ((low, ~has, ~has_c), (up, has, has_c)):
            before = jnp.where(away_c & (cols[k] < rows[k]), 1, 0)
            rank = jnp.sum(before, axis=0, keepdims=True)
            before_c = jnp.where(away & (rows[k] < cols[k]), 1, 0)
            rank_c = jnp.sum(before_c, axis=1, keepdims=True)
            chosen = away_c & (rank_c == lane)
            listed = jnp.sum(jnp.where(chosen, far * count + sub, 0), axis=0, keepdims=True)
            idx[12 + k : 13 + k, 0:count] = listed
            spot.append(rank)
            if k == low:
                traces = jnp.where(chosen, cols[k] - base, 0)
                idx[17 + axis : 18 + axis, 0:count] = jnp.sum(traces, axis=0, keepdims=True)
        first = face_dev + (0 if axis == 0 else nx)
        idx[far : far + 1, 0:count] = slots + jnp.where(has, starts[up] + spot[1], starts[low] + spot[0])
        idx[6 + far : 7 + far, 0:count] = jnp.where(has, first + spot[1], rows[low] - base)
        owned = (cols[low] - base) == wide
        slot_c = jnp.where(has_c, near, far) * count + wide_sub
        inverse = inverse + jnp.sum(jnp.where(owned, slot_c, 0), axis=0, keepdims=True)
    idx[16:17, :] = inverse
    idx[0:4, :] = jnp.clip(idx[0:4, :], 0, slots - 1)
    idx[4:6, :] = jnp.clip(idx[4:6, :], slots, slots + 2 * (nx + ny) - 1)
    idx[6:12, :] = jnp.clip(idx[6:12, :], 0, face_dev + nx + ny - 1)
    idx[12:17, :] = jnp.clip(idx[12:17, :], 0, slots - 1)
    idx[17:19, :] = jnp.clip(idx[17:19, :], 0, face_dev - 1)
    idx[19:20, :] = jnp.clip(idx[19:20, :], 0, 1)
    idx[20:21, :] = jnp.clip(idx[20:21, :], 2, 3)


def make_kernel(outer, inner, count, face_dev, groups, nx, ny):
    slots = 6 * count
    parts = outer * inner

    def kernel(heat_hbm, faces_hbm, stiff_ref,
               fin0, fin1, fin2, fin3, coef0, coef1, coef2, coef3, coef4, coef5, coef6,
               heat_ref, faces_ref, raw, high, low, diag, table, v0, v1, v2, flux, flux2, flux3, partial,
               idx_v, idx, send0, recv0, sends, recv1, recv2, recv3, sum_tx, sum_rx,
               fin,
               in_sem, out_sem, raw_sem, idx_sem, s0_sem, r0_sem, ss_sem, rr_sem,
               sum_ss, sum_rs):
        gx = lax.axis_index("gx")
        gy = lax.axis_index("gy")
        x_next = (lax.rem(gx + 1, outer), gy)
        x_prev = (lax.rem(gx + outer - 1, outer), gy)
        y_next = (gx, lax.rem(gy + 1, inner))
        y_prev = (gx, lax.rem(gy + inner - 1, inner))
        recvs = (recv1, recv2, recv3)

        get_heat = pltpu.make_async_copy(heat_hbm, heat_ref, in_sem.at[0])
        get_faces = pltpu.make_async_copy(faces_hbm, faces_ref, in_sem.at[1])
        get_faces.start()
        get_heat.start()

        def other(d):
            return (lax.rem(gx + d // inner, outer), lax.rem(gy + d % inner, inner))

        def raw_copy(e):
            return pltpu.make_async_copy(stiff_ref.at[e], raw.at[e], raw_sem.at[e])

        for e in range(count):
            raw_copy(e).start()
        barrier = pltpu.get_barrier_semaphore()
        for d in range(1, parts):
            pl.semaphore_signal(barrier, inc=1, device_id=other(d), device_id_type=MESH)

        base = (gx * inner + gy) * face_dev
        get_faces.wait()
        index_tables(faces_ref[...], base, count, face_dev, nx, ny, idx_v)
        to_smem = pltpu.make_async_copy(idx_v, idx, idx_sem)
        to_smem.start()

        def rows_of(f):
            return pl.ds((f // 8) * groups * 8 + f % 8, groups, stride=8)

        lane = lax.broadcasted_iota(jnp.int32, (8, LANES), 1)
        sub = lax.broadcasted_iota(jnp.int32, (8, LANES), 0)
        left = lane < HALF
        shifted = lane - sub
        on_diag = lane % 8 == sub

        def swap(a):
            return pltpu.roll(a, HALF, 1)

        def split(e):
            raw_copy(e).wait()
            for c in range(3):
                acc = None
                for k in range(6):
                    a = raw[e, k * HALF : (k + 1) * HALF, c * LANES : (c + 1) * LANES]
                    if k // 2 == c:
                        pieces = []
                        for i in range(HALF // 8):
                            piece = a[8 * i : 8 * i + 8]
                            mask = shifted == (k % 2) * HALF + 8 * i
                            acc = piece if acc is None else jnp.where(mask, piece, acc)
                            pieces.append(jnp.where(mask, 0.0, piece))
                        a = jnp.concatenate(pieces, axis=0)
                    h = a.astype(BF16)
                    high[e, c, k] = h
                    low[e, c, k] = (a - h.astype(F32)).astype(BF16)
                d = jnp.broadcast_to(
                    jnp.sum(jnp.where(on_diag, acc, 0.0), axis=0, keepdims=True), (8, LANES)
                )
                turned = swap(d)
                diag[e, 2 * c] = jnp.where(left, d, turned)
                diag[e, 2 * c + 1] = jnp.where(left, turned, d)

        def split_only(e, carry):
            split(e)
            return carry

        lax.fori_loop(0, AHEAD, split_only, 0, unroll=True)

        get_heat.wait()
        gamma0 = jnp.zeros((8, LANES), F32)
        for f in range(face_dev):
            t = heat_ref[rows_of(f), :]
            table[f] = t
            gamma0 = gamma0 + t * t
        to_smem.wait()

        def remote(src, dst, ssem, rsem, device):
            return pltpu.make_async_remote_copy(
                src_ref=src, dst_ref=dst, send_sem=ssem, recv_sem=rsem,
                device_id=device, device_id_type=MESH,
            )

        first = [
            remote(send0.at[pl.ds(0, nx)], recv0.at[pl.ds(0, nx)], s0_sem.at[0], r0_sem.at[0], x_prev),
            remote(send0.at[pl.ds(nx, ny)], recv0.at[pl.ds(nx, ny)], s0_sem.at[1], r0_sem.at[1], y_prev),
        ]
        def halves_of(tiles):
            evens, odds = [], []
            for a, b in zip(tiles[0::2], tiles[1::2]):
                evens.append(jnp.where(left, a, swap(b)))
                odds.append(jnp.where(left, swap(a), b))
            if len(evens) > 1:
                evens, odds = [jnp.concatenate(evens, axis=1)], [jnp.concatenate(odds, axis=1)]
            x = jnp.concatenate([evens[0], odds[0]], axis=0)
            xh = x.astype(BF16)
            return xh, (x - xh.astype(F32)).astype(BF16)

        def weights(ref, e, ks):
            return jnp.concatenate(
                [jnp.concatenate([ref[e, c, k] for k in ks], axis=0) for c in range(3)], axis=1
            )

        def near_product(tiles, e):
            xh, xl = halves_of(tiles)
            ks = (4, 5, idx[19, e], idx[20, e])
            both = jnp.concatenate([xh, xl], axis=0)
            p = jnp.dot(both, weights(high, e, ks), preferred_element_type=F32)
            q = jnp.dot(xh, weights(low, e, ks), preferred_element_type=F32)
            partial[e] = p[0:16] + (p[16:32] + q)

        def far_product(new, tiles, full, e, dot):
            xh, xl = halves_of(tiles)
            kx, ky = idx[19, e], idx[20, e]
            ks = (1 - kx, 5 - ky)
            both = jnp.concatenate(
                [jnp.concatenate([xh, xh], axis=1),
                 jnp.concatenate([xl, jnp.zeros_like(xl)], axis=1)], axis=0
            )
            w = jnp.concatenate([weights(high, e, ks), weights(low, e, ks)], axis=0)
            p = jnp.dot(both, w, preferred_element_type=F32)
            y = partial[e] + (p[0:16] + p[16:32])
            out = []
            for axis in range(3):
                part = y[:, axis * LANES : (axis + 1) * LANES]
                ev, od = part[0:8], part[8:16]
                out.append(jnp.where(left, ev, swap(od)))
                out.append(jnp.where(left, swap(ev), od))
            by_role = [
                out[4], out[5],
                jnp.where(kx == 0, out[0], out[1]), jnp.where(ky == 2, out[2], out[3]),
                jnp.where(kx == 0, out[1], out[0]), jnp.where(ky == 2, out[3], out[2]),
            ]
            kinds = (4, 5, kx, ky, *ks)
            for role in range(6):
                f = by_role[role] + full[role] * diag[e, kinds[role]]
                new[role * count + e] = f
                if dot is not None:
                    dot = dot + f * full[role]
            return dot

        spots = [0, nx, 2 * nx, 2 * nx + ny]
        plan = [(0, nx, x_prev, 1), (1, nx, x_next, 0), (2, ny, y_prev, 3), (3, ny, y_next, 2)]

        def exchange(phase, flux, kinds):
            copies = []
            for kind, rows, target, lands in plan:
                if kind not in kinds:
                    continue
                for r in range(rows):
                    sends[phase, spots[kind] + r] = flux[idx[12 + kind, r]]
                copies.append(
                    remote(
                        sends.at[phase, pl.ds(spots[kind], rows)],
                        recvs[phase].at[pl.ds(spots[lands], rows)],
                        ss_sem.at[phase, kind], rr_sem.at[phase, lands], target,
                    )
                )
                copies[-1].start()
            return copies

        def halves(tile):
            even = jnp.sum(jnp.where(left, tile, 0.0), axis=1, keepdims=True)
            odd = jnp.sum(jnp.where(left, 0.0, tile), axis=1, keepdims=True)
            return even, odd

        spot = lane % 16
        mine = lane // 16 == sub

        def packed(tiles):
            out = jnp.zeros((8, LANES), F32)
            for m, t in enumerate(tiles):
                even, odd = halves(t)
                out = jnp.where(spot == 2 * m, even, out)
                out = jnp.where(spot == 2 * m + 1, odd, out)
            return out

        def unpacked(row, m):
            own = jnp.where(mine, jnp.broadcast_to(row, (8, LANES)), 0.0)
            even = jnp.sum(jnp.where(spot == 2 * m, own, 0.0), axis=1, keepdims=True)
            odd = jnp.sum(jnp.where(spot == 2 * m + 1, own, 0.0), axis=1, keepdims=True)
            return jnp.where(left, even, odd)

        def sum_start(turn, value):
            sum_tx[turn] = jnp.sum(jnp.where(mine, value, 0.0), axis=0, keepdims=True)
            copies = []
            for d in range(1, parts):
                copies.append(remote(sum_tx.at[turn], sum_rx.at[turn, d - 1], sum_ss.at[turn, d - 1],
                                     sum_rs.at[turn, d - 1], other(d)))
                copies[-1].start()
            return copies

        def sum_end(turn, copies):
            for c in copies:
                c.wait_recv()
            return sum_tx[turn] + jnp.sum(sum_rx[turn], axis=0)

        zero = jnp.zeros((8, LANES), F32)
        every = (0, 1, 2, 3)

        def near_zero(e):
            tiles = []
            for role in range(4):
                t = table[idx[6 + role, e]]
                v0[role * count + e] = t
                tiles.append(t)
            near_product(tiles, e)

        def far_zero(e, dot):
            full = [v0[role * count + e] for role in range(4)]
            for role in (4, 5):
                t = table[idx[6 + role, e]]
                v0[role * count + e] = t
                full.append(t)
            return far_product(flux, full[4:], full, e, dot)

        lag = AHEAD - 1

        def near_step(e, carry):
            split(e)
            near_zero(e - lag)
            return carry

        def near_last(e, carry):
            near_zero(e)
            return carry

        near_zero(0)
        lax.fori_loop(AHEAD, MIDDLE, near_step, 0, unroll=True)
        for r in range(nx):
            send0[r] = table[idx[17, r]]
        for r in range(ny):
            send0[nx + r] = table[idx[18, r]]
        pl.semaphore_wait(barrier, parts - 1)
        for c in first:
            c.start()
        lax.fori_loop(MIDDLE, count, near_step, 0, unroll=True)
        lax.fori_loop(count - lag, count, near_last, 0, unroll=True)
        for c in first:
            c.wait_recv()
        for r in range(nx + ny):
            table[face_dev + r] = recv0[r]
        delta0 = lax.fori_loop(0, count, far_zero, zero, unroll=True)
        swap1 = exchange(0, flux, every)
        sum1 = sum_start(0, packed([gamma0, delta0]))

        def apply(v, old, recv, new, copies):
            def near(e, carry):
                tiles = []
                for role in range(4):
                    at = role * count + e
                    t = old[at] + old[idx[role, e]]
                    v[at] = t
                    tiles.append(t)
                near_product(tiles, e)
                return carry

            def far(e, carry):
                full = [v[role * count + e] for role in range(4)]
                for role in (4, 5):
                    at = role * count + e
                    t = old[at] + recv[idx[role, e] - slots]
                    v[at] = t
                    full.append(t)
                far_product(new, full[4:], full, e, None)
                return carry

            lax.fori_loop(0, count, near, 0, unroll=True)
            for c in copies:
                c.wait_recv()
            lax.fori_loop(0, count, far, 0, unroll=True)

        apply(v1, flux, recv1, flux2, swap1)
        swap2 = exchange(1, flux2, every)
        apply(v2, flux2, recv2, flux3, swap2)
        swap3 = exchange(2, flux3, (1, 3))
        total = sum_end(0, sum1)
        gamma0 = unpacked(total, 0)
        delta0 = unpacked(total, 1)
        alpha0 = gamma0 / delta0
        inverse0 = delta0 / gamma0

        def inner_products(e, carry):
            dot, once, twice = carry
            for role in range(6):
                at = role * count + e
                one = v1[at]
                w = one - alpha0 * v2[at]
                dot = dot + (flux2[at] - alpha0 * flux3[at]) * w
                if role == 1:
                    continue
                r1 = v0[at] - alpha0 * one
                terms = (r1 * r1, r1 * w, w * w)
                if role == 0:
                    once = tuple(a + t for a, t in zip(once, terms))
                else:
                    twice = tuple(a + t for a, t in zip(twice, terms))
            return dot, once, twice

        dot_e, once, twice = lax.fori_loop(
            0, count, inner_products, (zero, (zero,) * 3, (zero,) * 3), unroll=4
        )
        dots = [a + 0.5 * b for a, b in zip(once, twice)]
        sum2 = sum_start(1, packed([*dots, dot_e]))
        for c in swap3:
            c.wait_recv()
        for kind, rows, _, _ in plan:
            if kind in (0, 2):
                for r in range(rows):
                    flux3[slots + spots[kind] + r] = recv3[spots[kind] + r]

        def gather(fc, carry):
            at = idx[16, fc]
            pair = idx[lax.div(at, count), lax.rem(at, count)]
            x0, one, two = v0[at], v1[at], v2[at]
            rows = rows_of(fc)
            fin[0, rows, :] = x0
            fin[1, rows, :] = x0 - alpha0 * one
            fin[2, rows, :] = one - alpha0 * two
            fin[3, rows, :] = two - alpha0 * (flux3[at] + flux3[pair])
            return carry

        lax.fori_loop(0, face_dev, gather, 0, unroll=4)
        puts = [
            pltpu.make_async_copy(fin.at[m], to, out_sem.at[m])
            for m, to in enumerate((fin0, fin1, fin2, fin3))
        ]
        for c in puts:
            c.start()
        for c in [*first, *swap1, *swap2, *swap3, *sum1, *sum2]:
            c.wait_send()
        for c in puts:
            c.wait()

        total = sum_end(1, sum2)
        g1, d1, ww, ee = [unpacked(total, m) for m in range(4)]
        rv = -g1 * inverse0
        wv = (rv - d1) * inverse0
        vv = (delta0 - rv) * inverse0
        f = (wv - ww) * inverse0
        g = (vv - wv) * inverse0
        b0 = g1 / gamma0
        pap = d1 + 2.0 * b0 * rv + b0 * b0 * delta0
        a1 = g1 / pap
        rs = d1 + b0 * rv
        s2 = ww + b0 * (2.0 * wv + b0 * vv)
        g2 = g1 - 2.0 * a1 * rs + a1 * a1 * s2
        b1 = g2 / g1
        rar = d1 - 2.0 * a1 * (ww + b0 * wv) + a1 * a1 * (ee + b0 * (2.0 * f + b0 * g))
        pap2 = rar + 2.0 * b1 * (rs - a1 * s2) + b1 * b1 * pap
        a2 = g2 / pap2
        back = a1 * b0 * inverse0
        turn = b1 * b0 - back
        mixed = 1.0 + back + b1
        shift = a2 * turn * inverse0
        scales = (
            alpha0 + a1 * b0 + a2 * turn, a1 + a2 * mixed, -a2 * a1,
            -back - shift, 1.0 + back + shift, -a1 - a2 * mixed, a2 * a1,
        )
        for to, value in zip((coef0, coef1, coef2, coef3, coef4, coef5, coef6), scales):
            to[...] = value

    return kernel


def local(heat_source, stiffness, element_faces):
    face_dev, width = heat_source.shape
    count, order = stiffness.shape[0], stiffness.shape[1]
    groups = width // LANES
    outer = lax.axis_size("gx")
    inner = lax.axis_size("gy")
    nx, ny = EY * EZ, EX * EZ
    slots = 6 * count
    ext = 2 * (nx + ny)
    tile = (groups, LANES)
    flat = (face_dev * groups, LANES)
    vmem = lambda *s: pltpu.VMEM(s, F32)
    dma = lambda *s: pltpu.SemaphoreType.DMA(s)
    tiled = heat_source.reshape(face_dev // 8, 8, groups, LANES).transpose(0, 2, 1, 3)
    outs = pl.pallas_call(
        make_kernel(outer, inner, count, face_dev, groups, nx, ny),
        name="cg",
        out_shape=(
            *(jax.ShapeDtypeStruct(flat, F32),) * 4,
            *(jax.ShapeDtypeStruct(tile, F32),) * 7,
        ),
        in_specs=[
            pl.BlockSpec(memory_space=pltpu.HBM),
            pl.BlockSpec(memory_space=pltpu.HBM),
            pl.BlockSpec(memory_space=pltpu.HBM),
        ],
        out_specs=(
            *(pl.BlockSpec(memory_space=pltpu.HBM),) * 4,
            *(pl.BlockSpec(memory_space=pltpu.VMEM),) * 7,
        ),
        scratch_shapes=[
            vmem(*flat),
            pltpu.VMEM((6, count), jnp.int32),
            vmem(count, order, order),
            pltpu.VMEM((count, 3, 6, HALF, LANES), BF16),
            pltpu.VMEM((count, 3, 6, HALF, LANES), BF16),
            vmem(count, 6, 8, LANES),
            vmem(face_dev + nx + ny, *tile),
            vmem(slots, *tile),
            vmem(slots, *tile),
            vmem(slots, *tile),
            vmem(slots, *tile),
            vmem(slots, *tile),
            vmem(slots + ext, *tile),
            vmem(count, 16, order),
            pltpu.VMEM((24, LANES), jnp.int32),
            pltpu.SMEM((24, LANES), jnp.int32),
            vmem(nx + ny, *tile),
            vmem(nx + ny, *tile),
            vmem(3, ext, *tile),
            vmem(ext, *tile),
            vmem(ext, *tile),
            vmem(ext, *tile),
            vmem(2, 1, LANES),
            vmem(2, outer * inner - 1, 1, LANES),
            vmem(4, *flat),
            dma(2), dma(4),
            dma(count), pltpu.SemaphoreType.DMA,
            dma(2), dma(2), dma(3, 4), dma(3, 4),
            dma(2, outer * inner - 1), dma(2, outer * inner - 1),
        ],
        compiler_params=pltpu.CompilerParams(
            collective_id=0, has_side_effects=True, vmem_limit_bytes=67043328
        ),
    )(tiled.reshape(flat), element_faces.T, stiffness)

    x0, r1, w, last = [a.reshape(face_dev // 8, groups, 8, LANES) for a in outs[:4]]
    c = [a.reshape(1, groups, 1, LANES) for a in outs[4:]]

    def untile(a):
        return a.transpose(0, 2, 1, 3).reshape(face_dev, width)

    sol = c[0] * x0 + c[1] * r1 + c[2] * w
    res = c[3] * x0 + c[4] * r1 + c[5] * w + c[6] * last
    return untile(sol), untile(res)


def solution(mesh):
    return jax.shard_map(
        local,
        mesh=mesh,
        in_specs=(P(("gx", "gy"), None), P(("gx", "gy"), None, None), P(("gx", "gy"), None)),
        out_specs=(P(("gx", "gy"), None), P(("gx", "gy"), None)),
        check_vma=False,
    )
```

time: 33.3 us -> 32.7 us (0.982)
  other arithmetic: 0 us -> 2.07 us
  local copies, waits for them, and re-layouts: 1.84 us -> 0 us
  Pallas kernels: 30.7 us -> 29.9 us
    reshape x0 -> x1, other arithmetic: none -> 2.07 us  [untile(): return a.transpose(0, 2, 1, 3).reshape(face_dev, width)]
    reshape x1 -> x0, local copies, waits for them, and re-layouts: 1.84 us -> none  [local(): return (sol.reshape(face_dev, width), res.reshape(face_dev, width))]
    pallas_call x1, Pallas kernels: 30.7 us -> 29.9 us  [local(): pl.pallas_call(make_kernel(outer, inner, count, face_dev, groups, nx, ny)...]
where the time goes in v1:
time: 32.7 us; the launch traced here: 32.6 us
  Pallas kernels  29.9 us (91%)
  other arithmetic  2.07 us (6%)
  between operations  0.64 us (2%)
    pallas_call x1, Pallas kernels, local(): pl.pallas_call(make_kernel(outer, inner, count, face_dev, groups, nx, ny)...  29.9 us
    reshape x1, other arithmetic, untile(): return a.transpose(0, 2, 1, 3).reshape(face_dev, width)  2.07 us

profile of v1, /device:TPU:0, one launch (start us, length us, event | category | flops | bytes accessed | tf_op | source)
XLA Modules:
  0.0 32.6 jit_solution(9636349930393006661)
XLA Ops:
  0.6 29.9 %cg.1 = (f32[384,128]{1,0:T(8,128)}, f32[384,128]{1,0:T(8,128)}, f32[384,128]{1,0:T(8,128)}, f32[384,128]{1,0:T(8,128)}, f32[8,128]{1,0:T(8,128)}, /*index=5*/f3...) custom-call(f32[384,128]{1,0:T(8,128)} %bitcast.22, ...), custom_call_target="tpu_custom_call" | custom-call | tf_op jit(solution)/shard_map/cg/pallas_call | solution.py:473
  30.5 2.1 %add_bitcast_fusion = (f32[48,1024]{1,0:T(8,128)}, f32[48,1024]{1,0:T(8,128)}) fusion(f32[6,8,8,128]{3,2,1,0:T(8,128)} %bitcast.21, f32[6,8,8,128]{3,2,1,0:T(8,128)} %bitcast.20, f32[6,8,8,128]{3,2,1,0:T(8,128)} %bitcast.19, f32[6,8,8,128]{3,2,1,0:T(8,128)} %bitcast.18, f32[8,128]{1,0:T(8,128)} %get-tuple-element.22, f32[8,128]{1,0:T(8,128)} %get-tuple-element.21, ...), kind=kLoop, calls=%fused_computation | loop fusion | flops 589824 | bytes 1208320 | tf_op jit(solution)/shard_map/reshape | solution.py:529
